TPU v7x, 32 devices: a whole 2x2x4 slice. The times are simulated.
32 devices in a mesh: lat: 4 (over y, core), lon: 8 (over z, x).
Axes of the slice: x: 2, y: 2, z: 4, core: 2. Of those that a mesh axis runs over, the one named last changes fastest.
Arguments:
- state: float32 [4, 8, 448, 4096], P(None, None, 'lat', 'lon'), may hold values from -6 to 6
- level_courant: float32 [8], replicated, may hold values from 0.05 to 0.3
- damp_table: float32 [16, 2048], replicated, may hold values from 0.05 to 1
- row_flag: int32 [448], P('lat'), may hold values from 0 to 1, as said below
- row_table: int32 [448], P('lat'), may hold values from 0 to 15
- partner: int32 [4096], P('lon'), may hold values from 0 to 4095, each once
Outputs:
- new_state: float32 [4, 8, 448, 4096], P(None, None, 'lat', 'lon')
Inputs may be any that keep to these rules, and one draw needn't show every extreme that they name: `row_flag`: 0 on every row from 112 to 335; each row of the outer quarters is 1 or 0 on its own; the first and the last row are 1. `partner`: a permutation of the columns.
All inputs are finite; a program needn't handle non-finite values.
Results may differ from a plain program's by a relative error of at most 0.00005.
Values sent between devices are 32-bit elements; how exact they have to be, the bound alone decides.
A program may use at most 128 MiB of HBM per device.

v0:
```python
import math
import jax
import jax.numpy as jnp
from jax import lax
from jax.sharding import PartitionSpec as P

coriolis = 0.3
cos_floor = 0.25


def extended(cells, sides, width, closed):
    for axis, dim in sides:
        count = lax.axis_size(axis)
        ends = count if closed else count - 1
        head = lax.slice_in_dim(cells, 0, width, axis=dim)
        tail = lax.slice_in_dim(cells, cells.shape[dim] - width, cells.shape[dim], axis=dim)
        cells = jnp.concatenate(
            [
                lax.ppermute(tail, axis, [(i, (i + 1) % count) for i in range(ends)]),
                cells,
                lax.ppermute(head, axis, [((i + 1) % count, i) for i in range(ends)]),
            ],
            axis=dim,
        )
    return cells


def zonal_pair(stack):
    padded = extended(stack, (("lon", 3),), 1, True)
    return (padded[..., 2:], padded[..., :-2])


def meridional(stack, sign, partner):
    padded = extended(stack, (("lat", 2),), 1, False)
    edge_rows = jnp.concatenate([stack[:, :, :1, :], stack[:, :, -1:, :]], axis=2)
    circle = lax.all_gather(edge_rows, "lon", axis=3, tiled=True)
    across = sign * jnp.take(circle, partner, axis=3)
    southward = padded[:, :, :-2, :]
    northward = padded[:, :, 2:, :]
    at_south = lax.axis_index("lat") == 0
    at_north = lax.axis_index("lat") == lax.axis_size("lat") - 1
    southward = southward.at[:, :, 0, :].set(
        jnp.where(at_south, across[:, :, 0, :], southward[:, :, 0, :])
    )
    northward = northward.at[:, :, -1, :].set(
        jnp.where(at_north, across[:, :, 1, :], northward[:, :, -1, :])
    )
    return (northward, southward)


def angle_table(size_a, size_b, modulus):
    product = (
        jnp.arange(size_a, dtype=jnp.int32)[:, None]
        * jnp.arange(size_b, dtype=jnp.int32)[None, :]
        % modulus
    )
    angle = product.astype(jnp.float32) * (2.0 * math.pi / modulus)
    return (jnp.cos(angle), jnp.sin(angle))


def fourier_damp(rows_in, damping):
    count_b, count_r, length = rows_in.shape
    inner_len = 128
    outer_len = length // inner_len
    highest = lax.Precision.HIGHEST
    small_cos, small_sin = angle_table(outer_len, outer_len, outer_len)
    twid_cos, twid_sin = angle_table(outer_len, inner_len, length)
    large_cos, large_sin = angle_table(inner_len, inner_len, inner_len)
    grid = rows_in.reshape(count_b, count_r, outer_len, inner_len)
    a_real = jnp.einsum("brpq,kp->brkq", grid, small_cos, precision=highest)
    a_imag = -jnp.einsum("brpq,kp->brkq", grid, small_sin, precision=highest)
    b_real = a_real * twid_cos + a_imag * twid_sin
    b_imag = a_imag * twid_cos - a_real * twid_sin
    f_real = jnp.einsum("brkq,qm->brkm", b_real, large_cos, precision=highest) + jnp.einsum(
        "brkq,qm->brkm", b_imag, large_sin, precision=highest
    )
    f_imag = jnp.einsum("brkq,qm->brkm", b_imag, large_cos, precision=highest) - jnp.einsum(
        "brkq,qm->brkm", b_real, large_sin, precision=highest
    )
    weight = jnp.transpose(damping.reshape(count_r, inner_len, outer_len), (0, 2, 1))[None]
    f_real = f_real * weight
    f_imag = f_imag * weight
    z_real = jnp.einsum("brkq,qm->brkm", f_real, large_cos, precision=highest) - jnp.einsum(
        "brkq,qm->brkm", f_imag, large_sin, precision=highest
    )
    z_imag = jnp.einsum("brkq,qm->brkm", f_imag, large_cos, precision=highest) + jnp.einsum(
        "brkq,qm->brkm", f_real, large_sin, precision=highest
    )
    w_real = z_real * twid_cos - z_imag * twid_sin
    w_imag = z_imag * twid_cos + z_real * twid_sin
    result = jnp.einsum("brkq,kp->brpq", w_real, small_cos, precision=highest) - jnp.einsum(
        "brkq,kp->brpq", w_imag, small_sin, precision=highest
    )
    return (result / length).reshape(count_b, count_r, length)


def damp_half(values, row_codes, damp_table):
    active = jnp.any(row_codes > 0)

    def run_filter(inputs):
        table_count = damp_table.shape[0]
        row_count = row_codes.shape[0]
        pick = (row_codes[:, None] - 1 == jnp.arange(table_count, dtype=jnp.int32)[None, :]).astype(
            jnp.float32
        )
        half_damp = jnp.dot(
            pick, damp_table, precision=lax.Precision.HIGHEST, preferred_element_type=jnp.float32
        )
        full_damp = jnp.concatenate(
            [jnp.ones((row_count, 1), jnp.float32), half_damp, jnp.flip(half_damp[:, :-1], axis=1)],
            axis=1,
        )
        shaped = fourier_damp(inputs, full_damp)
        return jnp.where((row_codes > 0)[None, :, None], shaped, inputs)

    return lax.cond(active, run_filter, lambda kept: kept, values)


def regroup(row_block, row_codes, damp_table):
    fields_n, levels_n, rows_n, cols_n = row_block.shape
    half_rows = rows_n // 2
    merged = row_block.reshape(fields_n * levels_n, rows_n, cols_n)
    circles = lax.all_to_all(merged, "lon", split_axis=0, concat_axis=2, tiled=True)
    first_part = damp_half(circles[:, :half_rows, :], row_codes[:half_rows], damp_table)
    second_part = damp_half(circles[:, half_rows:, :], row_codes[half_rows:], damp_table)
    joined = jnp.concatenate([first_part, second_part], axis=1)
    returned = lax.all_to_all(joined, "lon", split_axis=2, concat_axis=0, tiled=True)
    return returned.reshape(fields_n, levels_n, rows_n, cols_n)


def per_device(state, level_courant, damp_table, row_flag, row_table, partner):
    fields_n, levels_n, rows_n, cols_n = state.shape
    whole_rows = rows_n * lax.axis_size("lat")
    row_pos = (lax.axis_index("lat") * rows_n + jnp.arange(rows_n, dtype=jnp.int32)).astype(
        jnp.float32
    )
    latitude = -jnp.pi / 2 + jnp.pi * (row_pos + 0.5) / whole_rows
    cos_lat = jnp.cos(latitude)[:, None]
    sin_lat = jnp.sin(latitude)[:, None]
    metric = 1.0 / jnp.maximum(cos_lat, cos_floor)
    courant = level_courant[:, None, None]
    pressure, wind_u, wind_v, thermo = (state[0], state[1], state[2], state[3])
    scalars = jnp.stack([pressure, thermo])
    eastward, westward = zonal_pair(scalars)
    northward, southward = meridional(scalars, 1.0, partner)
    tend_u = -courant * metric * (eastward[0] - westward[0]) * 0.5 + coriolis * sin_lat * wind_v
    tend_v = -courant * (northward[0] - southward[0]) * 0.5 - coriolis * sin_lat * wind_u
    u_new = wind_u + tend_u
    v_new = wind_v + tend_v
    flux = v_new * cos_lat
    u_east, u_west = zonal_pair(u_new[None])
    f_north, f_south = meridional(flux[None], -1.0, partner)
    divergence = (
        courant * metric * ((u_east[0] - u_west[0]) * 0.5 + (f_north[0] - f_south[0]) * 0.5)
    )
    tend_t = (
        -courant * metric * u_new * (eastward[1] - westward[1]) * 0.5
        - courant * v_new * (northward[1] - southward[1]) * 0.5
    )
    increments = jnp.stack([-divergence, tend_u, tend_v, tend_t])
    row_codes = jnp.where(row_flag == 1, row_table + 1, 0)
    increments = regroup(increments, row_codes, damp_table)
    return state + increments


def solution(mesh):
    placed = (P(None, None, "lat", "lon"), P(), P(), P("lat"), P("lat"), P("lon"))
    return jax.shard_map(
        per_device,
        mesh=mesh,
        in_specs=placed,
        out_specs=P(None, None, "lat", "lon"),
        check_vma=False,
    )
```

profile of v0, /device:TPU:0, one launch (start us, length us, event | category | flops | bytes accessed | tf_op | source)
XLA Modules:
  0.0 609.3 jit_solution(8997078380388542498)
XLA Ops:
  9.7 6.0 collective-permute-start
  16.1 31.4 %all_gather.6 = f32[2,8,2,4096]{3,1,2,0:T(8,128)S(1)} all-gather(f32[2,8,2,512]{3,1,2,0:T(8,128)S(1)} %pad_maximum_fusion.14), channel_id=1, replica_groups=mesh['lat'=4,'lon'=8] {'lon'}, dimensions={3}, use_global_device_ids=true | all-gather | bytes 589824 | tf_op jit(solution)/shard_map/all_gather | solution.py:36
  47.5 7.9 %copy.330 = f32[2,8,2,4096]{1,2,3,0:T(2,128)} copy(f32[2,8,2,4096]{3,1,2,0:T(8,128)S(1)} %all_gather.6) | data formatting | bytes 1048576 | tf_op jit(solution)/shard_map/all_gather | solution.py:36
  55.5 5.5 gather_fusion
  63.7 6.4 %pad_maximum_fusion.4 = (f32[2,8,112,512]{3,2,1,0:T(8,128)}, f32[2,8,112,512]{3,2,1,0:T(8,128)}) fusion(f32[2,8,1,512]{3,2,1,0:T(1,128)S(1)} %collective-permute-done.4, f32[1,8,112,512]{3,2,1,0:T(8,128)} %copy-done.8, f32[1,8,112,512]{3,2,1,0:T(8,128)S(1)} %get-tuple-element.94, f32[2,8,1,512]{3,2,1,0:T(1,128)S(1)} %collective-permute-done.5), kind=kLoop, calls=%fused_computation.277 | loop fusion | flops 3670016 | bytes 11075584 | tf_op jit(solution)/shard_map/concatenate | solution.py:17
  73.6 5.4 broadcast_multiply_fusion
  84.7 30.7 %all_gather.7 = f32[1,8,2,4096]{3,1,2,0:T(8,128)S(1)} all-gather(f32[1,8,2,512]{3,1,2,0:T(8,128)S(1)} %pad_maximum_fusion.16), channel_id=1, replica_groups=mesh['lat'=4,'lon'=8] {'lon'}, dimensions={3}, use_global_device_ids=true | all-gather | bytes 294912 | tf_op jit(solution)/shard_map/all_gather | solution.py:36
  123.5 8.2 %fusion.262 = (f32[1,8,112,512]{3,2,1,0:T(8,128)}, f32[1,8,112,512]{3,2,1,0:T(8,128)S(1)}, f32[1,8,112,512]{3,2,1,0:T(8,128)}) fusion(f32[2,8,112,512]{3,2,1,0:T(8,128)} %scatter.15, f32[2,8,112,512]{3,2,1,0:T(8,128)} %scatter.14, f32[2,8,112,1]{3,2,1,0:T(8,128)} %copy.327, f32[1,8,112,512]{3,2,1,0:T(8,128)} %copy-done.8, ...), kind=kLoop, calls=%fused_computation.282 | loop fusion | flops 11010048 | bytes 18368480 | tf_op jit(solution)/shard_map/sub | solution.py:157
  140.7 9.7 %collective-permute-done.2 = f32[1,8,112,1]{3,2,1,0:T(8,128)S(1)} collective-permute-done((f32[1,8,112,1]{3,2,1,0:T(8,128)S(1)}, f32[1,8,112,1]{3,2,1,0:T(8,128)S(1)}, u32[]{:S(2)}, u32[]{:S(2)}) %collective-permute-start.2) | collective-permute-done | bytes 3616 | tf_op jit(solution)/shard_map/ppermute | solution.py:21
  165.4 156.9 %all-to-all-done = f32[32,112,512]{2,1,0:T(8,128)} async-done(((f32[32,112,512]{2,1,0:T(8,128)}), f32[32,112,512]{2,1,0:T(8,128)}, u32[]{:S(2)}, u32[]{:S(2)}) %all-to-all-start) | async-done | bytes 7340064 | tf_op jit(solution)/shard_map/all_to_all | solution.py:123
  330.6 76.1 %conditional.2 = (f32[4,56,4096]{1,0,2:T(4,128)}) conditional(s32[]{:T(128)} %convert_element_type.123, f32[4,56,4096]{2,1,0:T(8,128)} %get-tuple-element.92, (s32[56]{0:T(128)S(1)}, f32[4,56,4096]{2,1,0:T(8,128)}, f32[16,2048]{1,0:T(8,128)S(1)}) %tuple.62), branch_computations={%region_1.2_spmd, %region_2.3_spmd} | conditional | flops 12735988736 | bytes 230196096 | solution.py:116
  340.6 5.3 fusion.4
  350.8 7.7 %subtract_multiply_fusion = f32[4,56,32,128]{3,2,1,0:T(8,128)S(1)} fusion(f32[4,56,32,128]{3,2,1,0:T(8,128)} %fusion.4, f32[56,32,128]{2,1,0:T(8,128)S(1)} %copy.319, f32[32,4,56,128]{3,0,2,1:T(8,128)} %copy-done.2, f32[32,4,56,128]{3,0,2,1:T(8,128)} %copy-done, f32[32,128]{1,0:T(8,128)S(1)} %get-tuple-element.88, f32[32,128]{1,0:T(8,128)S(1)} %get-tuple-element.89), kind=kOutput, calls=%fused_computation.23 | convolution fusion | flops 1415020544 | bytes 15630336 | tf_op jit(solution)/shard_map/cond/branch_1_fun/brkq,qm->brkm/dot_general | solution.py:77
  392.4 5.6 broadcast_select_fusion
  398.0 8.3 %copy.357 = f32[4,56,4096]{1,0,2:T(4,128)} copy(f32[4,56,4096]{2,1,0:T(8,128)} %broadcast_select_fusion) | data formatting | bytes 7340032 | tf_op jit(solution)/shard_map/cond | solution.py:116
  406.7 75.8 %conditional.3 = (f32[4,56,4096]{1,0,2:T(4,128)}) conditional(s32[]{:T(128)} %convert_element_type.125, f32[4,56,4096]{2,1,0:T(8,128)} %get-tuple-element.93, (s32[56]{0:T(128)S(1)}, f32[4,56,4096]{2,1,0:T(8,128)}, f32[16,2048]{1,0:T(8,128)S(1)}) %tuple.63), branch_computations={%region_4.5_spmd, %region_5.6_spmd} | conditional | flops 12735988736 | bytes 230196096 | solution.py:116
  426.4 7.7 %subtract_multiply_fusion.1 = f32[4,56,32,128]{3,2,1,0:T(8,128)S(1)} fusion(f32[4,56,32,128]{3,2,1,0:T(8,128)} %fusion.134, f32[56,32,128]{2,1,0:T(8,128)S(1)} %copy.323, f32[32,4,56,128]{3,0,2,1:T(8,128)} %copy-done.6, f32[32,4,56,128]{3,0,2,1:T(8,128)} %copy-done.4, f32[32,128]{1,0:T(8,128)S(1)} %get-tuple-element.90, f32[32,128]{1,0:T(8,128)S(1)} %get-tuple-element.91), kind=kOutput, calls=%fused_computation.155 | convolution fusion | flops 1415020544 | bytes 15630336 | tf_op jit(solution)/shard_map/cond/branch_1_fun/brkq,qm->brkm/dot_general | solution.py:77
  458.4 5.3 multiply_bitcast_fusion.1
  468.5 5.6 broadcast_select_fusion.1
  474.1 8.2 %copy.359 = f32[4,56,4096]{1,0,2:T(4,128)} copy(f32[4,56,4096]{2,1,0:T(8,128)} %broadcast_select_fusion.1) | data formatting | bytes 7340032 | tf_op jit(solution)/shard_map/cond | solution.py:116
  482.5 8.2 %pad_maximum_fusion = f32[4,112,4096]{1,0,2:T(4,128)S(1)} fusion(f32[4,56,4096]{1,0,2:T(4,128)} %get-tuple-element.80, f32[4,56,4096]{1,0,2:T(4,128)} %get-tuple-element.79), kind=kLoop, calls=%fused_computation.266 | loop fusion | flops 1835008 | bytes 14680064 | tf_op jit(solution)/shard_map/concatenate | solution.py:126
  490.8 98.2 %all_to_all.33 = f32[4,112,4096]{1,0,2:T(4,128)} all-to-all(f32[4,112,4096]{1,0,2:T(4,128)S(1)} %pad_maximum_fusion), channel_id=1, replica_groups=mesh['lat'=4,'lon'=8] {'lon'}, dimensions={2} | all-to-all | bytes 14680064 | tf_op jit(solution)/shard_map/all_to_all | solution.py:127
  588.9 9.5 %copy.339 = f32[8,4,112,512]{3,2,1,0:T(8,128)} copy(f32[8,4,112,512]{2,1,3,0:T(4,128)} %bitcast.199) | data formatting | bytes 14680064 | tf_op jit(solution)/shard_map/all_to_all | solution.py:127
  598.5 10.6 %bitcast_add_fusion = f32[4,8,112,512]{3,2,1,0:T(8,128)} fusion(f32[4,8,112,512]{3,2,1,0:T(8,128)} %param.18, f32[4,8,112,512]{3,2,1,0:T(8,128)} %bitcast.206), kind=kLoop, calls=%fused_computation.268 | loop fusion | flops 1835008 | bytes 22020096 | tf_op jit(solution)/shard_map/add | solution.py:163
  (141 shorter events, 157.6 us)
Async XLA Ops:
  2.6 5.7 copy-start.8
  2.6 61.0 %collective-permute-start.4 = (f32[2,8,1,512]{3,2,1,0:T(1,128)S(1)}, f32[2,8,1,512]{3,2,1,0:T(1,128)S(1)}, u32[]{:S(2)}, u32[]{:S(2)}) collective-permute-start(f32[2,8,1,512]{3,2,1,0:T(1,128)S(1)} %get-tuple-element.100), channel_id=1, source_target_pairs={{8,0},{16,8},{24,16},{9,1},{17,9},{25,17},{10,2},{18,10},{26,18},{... | collective-permute-start | bytes 98312 | tf_op jit(solution)/shard_map/ppermute | solution.py:21
  3.9 12.1 %copy-start.16 = (s32[512]{0:T(512)S(1)}, s32[512]{0:T(512)}, u32[]{:S(2)}) copy-start(s32[512]{0:T(512)} %param.23) | copy-start | bytes 6148
  4.0 59.7 %collective-permute-start.5 = (f32[2,8,1,512]{3,2,1,0:T(1,128)S(1)}, f32[2,8,1,512]{3,2,1,0:T(1,128)S(1)}, u32[]{:S(2)}, u32[]{:S(2)}) collective-permute-start(f32[2,8,1,512]{3,2,1,0:T(1,128)S(1)} %get-tuple-element.101), channel_id=1, source_target_pairs={{0,8},{8,16},{16,24},{1,9},{9,17},{17,25},{2,10},{10,18},{18,26},{... | collective-permute-start | bytes 98312 | tf_op jit(solution)/shard_map/ppermute | solution.py:19
  9.7 52.3 %collective-permute-start = (f32[2,8,112,1]{2,1,3,0:T(8,128)S(1)}, f32[2,8,112,1]{2,1,3,0:T(8,128)S(1)}, u32[]{:S(2)}, u32[]{:S(2)}) collective-permute-start(f32[2,8,112,1]{2,1,3,0:T(8,128)S(1)} %copy.360), channel_id=1, source_target_pairs={{1,0},{2,1},{3,2},{4,3},{5,4},{6,5},{7,6},{0,7},{9,8},{10,9},{11,1... | collective-permute-start | bytes 21512 | tf_op jit(solution)/shard_map/ppermute | solution.py:21
  16.0 46.4 %collective-permute-start.1 = (f32[2,8,112,1]{2,1,3,0:T(8,128)S(1)}, f32[2,8,112,1]{2,1,3,0:T(8,128)S(1)}, u32[]{:S(2)}, u32[]{:S(2)}) collective-permute-start(f32[2,8,112,1]{2,1,3,0:T(8,128)S(1)} %copy.361), channel_id=1, source_target_pairs={{0,1},{1,2},{2,3},{3,4},{4,5},{5,6},{6,7},{7,0},{8,9},{9,10},{10,1... | collective-permute-start | bytes 21512 | tf_op jit(solution)/shard_map/ppermute | solution.py:19
  47.5 14.3 %copy-start.17 = (f32[8]{0:T(128)S(1)}, f32[8]{0:T(128)}, u32[]{:S(2)}) copy-start(f32[8]{0:T(128)} %param.19) | copy-start | bytes 100
  80.3 56.3 %collective-permute-start.6 = (f32[1,8,1,512]{3,2,1,0:T(1,128)S(1)}, f32[1,8,1,512]{3,2,1,0:T(1,128)S(1)}, u32[]{:S(2)}, u32[]{:S(2)}) collective-permute-start(f32[1,8,1,512]{3,2,1,0:T(1,128)S(1)} %get-tuple-element.105), channel_id=1, source_target_pairs={{8,0},{16,8},{24,16},{9,1},{17,9},{25,17},{10,2},{18,10},{26,18},{... | collective-permute-start | bytes 49160 | tf_op jit(solution)/shard_map/ppermute | solution.py:21
  81.6 55.0 %collective-permute-start.7 = (f32[1,8,1,512]{3,2,1,0:T(1,128)S(1)}, f32[1,8,1,512]{3,2,1,0:T(1,128)S(1)}, u32[]{:S(2)}, u32[]{:S(2)}) collective-permute-start(f32[1,8,1,512]{3,2,1,0:T(1,128)S(1)} %get-tuple-element.104), channel_id=1, source_target_pairs={{0,8},{8,16},{16,24},{1,9},{9,17},{17,25},{2,10},{10,18},{18,26},{... | collective-permute-start | bytes 49160 | tf_op jit(solution)/shard_map/ppermute | solution.py:19
  123.5 13.1 %copy-start.12 = (f32[1,8,112,512]{3,2,1,0:T(8,128)S(1)}, f32[1,8,112,512]{3,2,1,0:T(8,128)}, u32[]{:S(2)}) copy-start(f32[1,8,112,512]{3,2,1,0:T(8,128)} %copy-done.11) | copy-start | bytes 5505028
  131.8 6.6 %copy-start.10 = (f32[1,8,112,512]{3,2,1,0:T(8,128)}, f32[1,8,112,512]{3,2,1,0:T(8,128)S(1)}, u32[]{:S(2)}) copy-start(f32[1,8,112,512]{3,2,1,0:T(8,128)S(1)} %get-tuple-element.86) | copy-start | bytes 5505028
  132.0 18.4 %collective-permute-start.2 = (f32[1,8,112,1]{3,2,1,0:T(8,128)S(1)}, f32[1,8,112,1]{3,2,1,0:T(8,128)S(1)}, u32[]{:S(2)}, u32[]{:S(2)}) collective-permute-start(f32[1,8,112,1]{3,2,1,0:T(8,128)S(1)} %get-tuple-element.106), channel_id=1, source_target_pairs={{1,0},{2,1},{3,2},{4,3},{5,4},{6,5},{7,6},{0,7},{9,8},{10,9},{11,1... | collective-permute-start | bytes 10760 | tf_op jit(solution)/shard_map/ppermute | solution.py:21
  136.6 13.8 %collective-permute-start.3 = (f32[1,8,112,1]{3,2,1,0:T(8,128)S(1)}, f32[1,8,112,1]{3,2,1,0:T(8,128)}, u32[]{:S(2)}, u32[]{:S(2)}) collective-permute-start(f32[1,8,112,1]{3,2,1,0:T(8,128)S(1)} %get-tuple-element.107), channel_id=1, source_target_pairs={{0,1},{1,2},{2,3},{3,4},{4,5},{5,6},{6,7},{7,0},{8,9},{9,10},{10,1... | collective-permute-start | bytes 10760 | tf_op jit(solution)/shard_map/ppermute | solution.py:19
  150.4 4.2 copy-start.9
  150.4 4.2 copy-start.13
  150.4 4.4 copy-start.14
  158.2 5.1 copy-start.18
  158.2 5.1 copy-start.19
  158.2 164.2 %all-to-all-start = ((f32[32,112,512]{2,1,0:T(8,128)}), f32[32,112,512]{2,1,0:T(8,128)}, u32[]{:S(2)}, u32[]{:S(2)}) async-start(f32[32,112,512]{2,1,0:T(8,128)} %bitcast.204), calls=%async_computation | async-start | bytes 14680064 | tf_op jit(solution)/shard_map/all_to_all | solution.py:123
  326.7 3.9 copy-start.15
  337.0 3.5 copy-start
  340.5 5.3 copy-start.2
  413.0 3.5 copy-start.4
  416.5 5.2 copy-start.6
  (5 other events, 14.3 us)
where the time goes:
time: 619 us; the launch traced here: 609 us
  waiting for transfers between devices  167 us (27%)
  blocking collectives  160 us (26%)
  matrix products  99.1 us (16%)
  local copies, waits for them, and re-layouts  93.7 us (15%)
  other arithmetic  62.2 us (10%)
  starting transfers between devices  24.4 us (4%)
    all_to_all x1, waiting for transfers between devices, regroup(): lax.all_to_all(merged, 'lon', split_axis=0, concat_axis=2, tiled=True)  157 us
    all_to_all x1, blocking collectives, regroup(): lax.all_to_all(joined, 'lon', split_axis=2, concat_axis=0, tiled=True)  98.2 us
    all_gather x2, blocking collectives, meridional(): circle = lax.all_gather(edge_rows, 'lon', axis=3, tiled=True)  62.2 us
    cond x2, local copies, waits for them, and re-layouts, damp_half(): return lax.cond(active, run_filter, lambda kept: kept, values)  16.6 us
    dot_general x2, matrix products, fourier_damp(): jnp.einsum('brkq,qm->brkm', b_real, large_sin, precision=highest)  15.4 us
    ppermute x4, starting transfers between devices, extended(): lax.ppermute(head, axis, [((i + 1) % count, i) for i in range(ends)])  13.2 us
  transfers between devices with their start and end apart: 9, of which 2 were waited for; matrix products, arithmetic and copies ran while one was open for 7% of the time, Pallas kernels for 0%

commit v1 on v0

--- a/solution.py
+++ b/solution.py
@@ -6,6 +6,19 @@
 
 coriolis = 0.3
 cos_floor = 0.25
+
+
+def stacks_all_register(sample, dim_at, point):
+    res, block_out = (sample.shape[:dim_at], sample.shape[dim_at + 1 :])
+    a_next = jnp.moveaxis(sample.reshape(*res, point, -1, *block_out), dim_at, 0)
+    return a_next
+
+
+def solve_record(xs, d_out):
+    xs = jnp.moveaxis(xs, 0, d_out)
+    d_next = xs.shape
+    oldest = xs.reshape(*d_next[:d_out], d_next[d_out] * d_next[d_out + 1], *d_next[d_out + 2 :])
+    return oldest
 
 
 def extended(cells, sides, width, closed):
@@ -117,10 +130,28 @@
 
 
 def regroup(row_block, row_codes, damp_table):
+
+    def _report_samples_all(local_values, which_axis, unit, array_in):
+        fresh = jax.lax.psum(1, which_axis)
+        step_out = jax.lax.axis_index(which_axis)
+        raw_out, arr_out = (fresh, step_out)
+        y2 = stacks_all_register(local_values, unit, raw_out)
+        tmp = y2
+        for s in tuple(range(1, raw_out)):
+            t_next, mid_arr = ((arr_out + s) % raw_out, (arr_out - s) % raw_out)
+            f_next = lax.dynamic_index_in_dim(y2, t_next, 0)
+            tray = []
+            for p in [*range(raw_out)]:
+                tray.append((p, (p + s) % raw_out))
+            local_out = jax.lax.ppermute(f_next, which_axis, tray)
+            tmp = lax.dynamic_update_slice_in_dim(tmp, local_out, mid_arr, axis=0)
+        q_next = solve_record(tmp, array_in)
+        return q_next
+
     fields_n, levels_n, rows_n, cols_n = row_block.shape
     half_rows = rows_n // 2
     merged = row_block.reshape(fields_n * levels_n, rows_n, cols_n)
-    circles = lax.all_to_all(merged, "lon", split_axis=0, concat_axis=2, tiled=True)
+    circles = _report_samples_all(merged, "lon", 0, 2)
     first_part = damp_half(circles[:, :half_rows, :], row_codes[:half_rows], damp_table)
     second_part = damp_half(circles[:, half_rows:, :], row_codes[half_rows:], damp_table)
     joined = jnp.concatenate([first_part, second_part], axis=1)

time: 619 us -> 647 us (1.045)
  blocking collectives: 160 us -> 206 us
  waiting for transfers between devices: 167 us -> 126 us
  local copies, waits for them, and re-layouts: 93.7 us -> 115 us
    all_to_all x1 -> x0, waiting for transfers between devices: 157 us -> none  [regroup(): lax.all_to_all(merged, 'lon', split_axis=0, concat_axis=2, tiled=True)]
    ppermute x0 -> x7, waiting for transfers between devices: none -> 116 us  [_report_samples_all(): local_out = jax.lax.ppermute(f_next, which_axis, tray)]
    all_to_all x1, blocking collectives: 98.2 us -> 144 us  [regroup(): lax.all_to_all(joined, 'lon', split_axis=2, concat_axis=0, tiled=True)]
    dynamic_update_slice x0 -> x6, local copies, waits for them, and re-layouts: none -> 13 us  [_report_samples_all(): tmp = lax.dynamic_update_slice_in_dim(tmp, local_out, mid_arr, axis=0)]
    ppermute x0 -> x7, starting transfers between devices: none -> 9.51 us  [_report_samples_all(): local_out = jax.lax.ppermute(f_next, which_axis, tray)]
  transfers between devices with their start and end apart: 9 -> 15, of which waited for: 2 -> 6; matrix products, arithmetic and copies ran while one was open for 7% -> 8% of each run, Pallas kernels for 0% -> 0%
where the time goes in v1:
time: 647 us; the launch traced here: 638 us
  blocking collectives  206 us (32%)
  waiting for transfers between devices  126 us (19%)
  local copies, waits for them, and re-layouts  115 us (18%)
  matrix products  99.1 us (15%)
  other arithmetic  59.7 us (9%)
  starting transfers between devices  28.8 us (4%)
    all_to_all x1, blocking collectives, regroup(): lax.all_to_all(joined, 'lon', split_axis=2, concat_axis=0, tiled=True)  144 us
    ppermute x7, waiting for transfers between devices, _report_samples_all(): local_out = jax.lax.ppermute(f_next, which_axis, tray)  116 us
    all_gather x2, blocking collectives, meridional(): circle = lax.all_gather(edge_rows, 'lon', axis=3, tiled=True)  62.2 us
    cond x2, local copies, waits for them, and re-layouts, damp_half(): return lax.cond(active, run_filter, lambda kept: kept, values)  16.6 us
    dot_general x2, matrix products, fourier_damp(): jnp.einsum('brkq,qm->brkm', b_real, large_sin, precision=highest)  15.4 us
    ppermute x4, starting transfers between devices, extended(): lax.ppermute(head, axis, [((i + 1) % count, i) for i in range(ends)])  13.2 us
    dynamic_update_slice x6, local copies, waits for them, and re-layouts, _report_samples_all(): tmp = lax.dynamic_update_slice_in_dim(tmp, local_out, mid_arr, axis=0)  13 us
  transfers between devices with their start and end apart: 15, of which 6 were waited for; matrix products, arithmetic and copies ran while one was open for 8% of the time, Pallas kernels for 0%

profile of v1, /device:TPU:0, one launch (start us, length us, event | category | flops | bytes accessed | tf_op | source)
XLA Modules:
  0.0 637.7 jit_solution(7423982656110976118)
XLA Ops:
  9.7 6.0 collective-permute-start
  16.1 31.4 %all_gather.6 = f32[2,8,2,4096]{3,1,2,0:T(8,128)S(1)} all-gather(f32[2,8,2,512]{3,1,2,0:T(8,128)S(1)} %pad_maximum_fusion.14), channel_id=1, replica_groups=mesh['lat'=4,'lon'=8] {'lon'}, dimensions={3}, use_global_device_ids=true | all-gather | bytes 589824 | tf_op jit(solution)/shard_map/all_gather | solution.py:49
  47.5 7.9 %copy.379 = f32[2,8,2,4096]{1,2,3,0:T(2,128)} copy(f32[2,8,2,4096]{3,1,2,0:T(8,128)S(1)} %all_gather.6) | data formatting | bytes 1048576 | tf_op jit(solution)/shard_map/all_gather | solution.py:49
  63.7 6.4 %pad_maximum_fusion.4 = (f32[2,8,112,512]{3,2,1,0:T(8,128)}, f32[2,8,112,512]{3,2,1,0:T(8,128)}) fusion(f32[2,8,1,512]{3,2,1,0:T(1,128)S(1)} %collective-permute-done.4, f32[1,8,112,512]{3,2,1,0:T(8,128)} %copy-done.9, f32[1,8,112,512]{3,2,1,0:T(8,128)S(1)} %get-tuple-element.101, f32[2,8,1,512]{3,2,1,0:T(1,128)S(1)} %collective-permute-done.5), kind=kLoop, calls=%fused_computation.277 | loop fusion | flops 3670016 | bytes 11075584 | tf_op jit(solution)/shard_map/concatenate | solution.py:30
  84.8 30.7 %all_gather.7 = f32[1,8,2,4096]{3,1,2,0:T(8,128)S(1)} all-gather(f32[1,8,2,512]{3,1,2,0:T(8,128)S(1)} %pad_maximum_fusion.16), channel_id=1, replica_groups=mesh['lat'=4,'lon'=8] {'lon'}, dimensions={3}, use_global_device_ids=true | all-gather | bytes 294912 | tf_op jit(solution)/shard_map/all_gather | solution.py:49
  123.6 8.2 %fusion.262 = (f32[1,8,112,512]{3,2,1,0:T(8,128)}, f32[1,8,112,512]{3,2,1,0:T(8,128)S(1)}, f32[1,8,112,512]{3,2,1,0:T(8,128)}) fusion(f32[2,8,112,512]{3,2,1,0:T(8,128)} %scatter.15, f32[2,8,112,512]{3,2,1,0:T(8,128)} %scatter.14, f32[2,8,112,1]{3,2,1,0:T(8,128)} %copy.376, f32[1,8,112,512]{3,2,1,0:T(8,128)} %copy-done.9, ...), kind=kLoop, calls=%fused_computation.282 | loop fusion | flops 11010048 | bytes 18368480 | tf_op jit(solution)/shard_map/sub | solution.py:188
  140.4 10.0 %collective-permute-done.2 = f32[1,8,112,1]{3,2,1,0:T(8,128)S(1)} collective-permute-done((f32[1,8,112,1]{3,2,1,0:T(8,128)S(1)}, f32[1,8,112,1]{3,2,1,0:T(8,128)S(1)}, u32[]{:S(2)}, u32[]{:S(2)}) %collective-permute-start.2) | collective-permute-done | bytes 3616 | tf_op jit(solution)/shard_map/ppermute | solution.py:34
  160.9 21.4 %collective-permute-done.8 = f32[1,4,112,512]{3,2,1,0:T(8,128)} collective-permute-done((f32[1,4,112,512]{3,2,1,0:T(8,128)S(1)}, f32[1,4,112,512]{3,2,1,0:T(8,128)}, u32[]{:S(2)}, u32[]{:S(2)}) %collective-permute-start.8) | collective-permute-done | bytes 917536 | tf_op jit(solution)/shard_map/ppermute | solution.py:146
  194.9 17.6 %collective-permute-done.9 = f32[1,4,112,512]{3,2,1,0:T(8,128)S(1)} collective-permute-done((f32[1,4,112,512]{3,2,1,0:T(8,128)S(1)}, f32[1,4,112,512]{3,2,1,0:T(8,128)S(1)}, u32[]{:S(2)}, u32[]{:S(2)}) %collective-permute-start.9) | collective-permute-done | bytes 917536 | tf_op jit(solution)/shard_map/ppermute | solution.py:146
  217.4 50.4 %collective-permute-done.10 = f32[1,4,112,512]{3,2,1,0:T(8,128)} collective-permute-done((f32[1,4,112,512]{3,2,1,0:T(8,128)}, f32[1,4,112,512]{3,2,1,0:T(8,128)}, u32[]{:S(2)}, u32[]{:S(2)}) %collective-permute-start.10) | collective-permute-done | bytes 917536 | tf_op jit(solution)/shard_map/ppermute | solution.py:146
  270.0 17.4 %collective-permute-done.11 = f32[1,4,112,512]{3,2,1,0:T(8,128)} collective-permute-done((f32[1,4,112,512]{3,2,1,0:T(8,128)}, f32[1,4,112,512]{3,2,1,0:T(8,128)}, u32[]{:S(2)}, u32[]{:S(2)}) %collective-permute-start.11) | collective-permute-done | bytes 917536 | tf_op jit(solution)/shard_map/ppermute | solution.py:146
  293.9 9.4 %collective-permute-done.14 = f32[1,4,112,512]{3,2,1,0:T(8,128)} collective-permute-done((f32[1,4,112,512]{3,2,1,0:T(8,128)S(1)}, f32[1,4,112,512]{3,2,1,0:T(8,128)}, u32[]{:S(2)}, u32[]{:S(2)}) %collective-permute-start.14) | collective-permute-done | bytes 917536 | tf_op jit(solution)/shard_map/ppermute | solution.py:146
  313.6 76.2 %conditional.2 = (f32[4,56,4096]{1,0,2:T(4,128)}) conditional(s32[]{:T(128)} %convert_element_type.123, f32[4,56,4096]{2,1,0:T(8,128)} %get-tuple-element.92, (s32[56]{0:T(128)S(1)}, f32[4,56,4096]{2,1,0:T(8,128)}, f32[16,2048]{1,0:T(8,128)S(1)}) %tuple.68), branch_computations={%region_1.2_spmd, %region_2.3_spmd} | conditional | flops 12735988736 | bytes 230196096 | solution.py:129
  333.9 7.7 %subtract_multiply_fusion = f32[4,56,32,128]{3,2,1,0:T(8,128)S(1)} fusion(f32[4,56,32,128]{3,2,1,0:T(8,128)} %fusion.4, f32[56,32,128]{2,1,0:T(8,128)S(1)} %copy.368, f32[32,4,56,128]{3,0,2,1:T(8,128)} %copy-done.2, f32[32,4,56,128]{3,0,2,1:T(8,128)} %copy-done, f32[32,128]{1,0:T(8,128)S(1)} %get-tuple-element.88, f32[32,128]{1,0:T(8,128)S(1)} %get-tuple-element.89), kind=kOutput, calls=%fused_computation.23 | convolution fusion | flops 1415020544 | bytes 15630336 | tf_op jit(solution)/shard_map/cond/branch_1_fun/brkq,qm->brkm/dot_general | solution.py:90
  375.5 5.6 broadcast_select_fusion
  381.1 8.3 %copy.406 = f32[4,56,4096]{1,0,2:T(4,128)} copy(f32[4,56,4096]{2,1,0:T(8,128)} %broadcast_select_fusion) | data formatting | bytes 7340032 | tf_op jit(solution)/shard_map/cond | solution.py:129
  389.8 75.8 %conditional.3 = (f32[4,56,4096]{1,0,2:T(4,128)}) conditional(s32[]{:T(128)} %convert_element_type.125, f32[4,56,4096]{2,1,0:T(8,128)} %get-tuple-element.93, (s32[56]{0:T(128)S(1)}, f32[4,56,4096]{2,1,0:T(8,128)}, f32[16,2048]{1,0:T(8,128)S(1)}) %tuple.69), branch_computations={%region_4.5_spmd, %region_5.6_spmd} | conditional | flops 12735988736 | bytes 230196096 | solution.py:129
  409.5 7.7 %subtract_multiply_fusion.1 = f32[4,56,32,128]{3,2,1,0:T(8,128)S(1)} fusion(f32[4,56,32,128]{3,2,1,0:T(8,128)} %fusion.134, f32[56,32,128]{2,1,0:T(8,128)S(1)} %copy.372, f32[32,4,56,128]{3,0,2,1:T(8,128)} %copy-done.6, f32[32,4,56,128]{3,0,2,1:T(8,128)} %copy-done.4, f32[32,128]{1,0:T(8,128)S(1)} %get-tuple-element.90, f32[32,128]{1,0:T(8,128)S(1)} %get-tuple-element.91), kind=kOutput, calls=%fused_computation.155 | convolution fusion | flops 1415020544 | bytes 15630336 | tf_op jit(solution)/shard_map/cond/branch_1_fun/brkq,qm->brkm/dot_general | solution.py:90
  451.6 5.6 broadcast_select_fusion.1
  457.2 8.2 %copy.408 = f32[4,56,4096]{1,0,2:T(4,128)} copy(f32[4,56,4096]{2,1,0:T(8,128)} %broadcast_select_fusion.1) | data formatting | bytes 7340032 | tf_op jit(solution)/shard_map/cond | solution.py:129
  465.6 8.2 %pad_maximum_fusion = f32[4,112,4096]{1,0,2:T(4,128)S(1)} fusion(f32[4,56,4096]{1,0,2:T(4,128)} %get-tuple-element.80, f32[4,56,4096]{1,0,2:T(4,128)} %get-tuple-element.79), kind=kLoop, calls=%fused_computation.266 | loop fusion | flops 1835008 | bytes 14680064 | tf_op jit(solution)/shard_map/concatenate | solution.py:157
  473.8 143.5 %all_to_all.15 = f32[4,112,4096]{1,0,2:T(4,128)} all-to-all(f32[4,112,4096]{1,0,2:T(4,128)S(1)} %pad_maximum_fusion), channel_id=1, replica_groups=mesh['lat'=4,'lon'=8] {'lon'}, dimensions={2} | all-to-all | bytes 14680064 | tf_op jit(solution)/shard_map/all_to_all | solution.py:158
  617.4 9.5 %copy.388 = f32[8,4,112,512]{3,2,1,0:T(8,128)} copy(f32[8,4,112,512]{2,1,3,0:T(4,128)} %bitcast.200) | data formatting | bytes 14680064 | tf_op jit(solution)/shard_map/all_to_all | solution.py:158
  626.9 10.6 %bitcast_add_fusion = f32[4,8,112,512]{3,2,1,0:T(8,128)} fusion(f32[4,8,112,512]{3,2,1,0:T(8,128)} %param.18, f32[4,8,112,512]{3,2,1,0:T(8,128)} %bitcast.206), kind=kLoop, calls=%fused_computation.268 | loop fusion | flops 1835008 | bytes 22020096 | tf_op jit(solution)/shard_map/add | solution.py:194
  (165 shorter events, 202.8 us)
Async XLA Ops:
  2.6 5.7 copy-start.9
  2.6 61.1 %collective-permute-start.4 = (f32[2,8,1,512]{3,2,1,0:T(1,128)S(1)}, f32[2,8,1,512]{3,2,1,0:T(1,128)S(1)}, u32[]{:S(2)}, u32[]{:S(2)}) collective-permute-start(f32[2,8,1,512]{3,2,1,0:T(1,128)S(1)} %get-tuple-element.107), channel_id=1, source_target_pairs={{8,0},{16,8},{24,16},{9,1},{17,9},{25,17},{10,2},{18,10},{26,18},{... | collective-permute-start | bytes 98312 | tf_op jit(solution)/shard_map/ppermute | solution.py:34
  3.9 12.1 %copy-start.18 = (s32[512]{0:T(512)S(1)}, s32[512]{0:T(512)}, u32[]{:S(2)}) copy-start(s32[512]{0:T(512)} %param.23) | copy-start | bytes 6148
  4.0 59.7 %collective-permute-start.5 = (f32[2,8,1,512]{3,2,1,0:T(1,128)S(1)}, f32[2,8,1,512]{3,2,1,0:T(1,128)S(1)}, u32[]{:S(2)}, u32[]{:S(2)}) collective-permute-start(f32[2,8,1,512]{3,2,1,0:T(1,128)S(1)} %get-tuple-element.108), channel_id=1, source_target_pairs={{0,8},{8,16},{16,24},{1,9},{9,17},{17,25},{2,10},{10,18},{18,26},{... | collective-permute-start | bytes 98312 | tf_op jit(solution)/shard_map/ppermute | solution.py:32
  9.7 52.3 %collective-permute-start = (f32[2,8,112,1]{2,1,3,0:T(8,128)S(1)}, f32[2,8,112,1]{2,1,3,0:T(8,128)S(1)}, u32[]{:S(2)}, u32[]{:S(2)}) collective-permute-start(f32[2,8,112,1]{2,1,3,0:T(8,128)S(1)} %copy.409), channel_id=1, source_target_pairs={{1,0},{2,1},{3,2},{4,3},{5,4},{6,5},{7,6},{0,7},{9,8},{10,9},{11,1... | collective-permute-start | bytes 21512 | tf_op jit(solution)/shard_map/ppermute | solution.py:34
  16.0 46.4 %collective-permute-start.1 = (f32[2,8,112,1]{2,1,3,0:T(8,128)S(1)}, f32[2,8,112,1]{2,1,3,0:T(8,128)S(1)}, u32[]{:S(2)}, u32[]{:S(2)}) collective-permute-start(f32[2,8,112,1]{2,1,3,0:T(8,128)S(1)} %copy.410), channel_id=1, source_target_pairs={{0,1},{1,2},{2,3},{3,4},{4,5},{5,6},{6,7},{7,0},{8,9},{9,10},{10,1... | collective-permute-start | bytes 21512 | tf_op jit(solution)/shard_map/ppermute | solution.py:32
  47.5 14.3 %copy-start.19 = (f32[8]{0:T(128)S(1)}, f32[8]{0:T(128)}, u32[]{:S(2)}) copy-start(f32[8]{0:T(128)} %param.19) | copy-start | bytes 100
  80.4 56.3 %collective-permute-start.6 = (f32[1,8,1,512]{3,2,1,0:T(1,128)S(1)}, f32[1,8,1,512]{3,2,1,0:T(1,128)S(1)}, u32[]{:S(2)}, u32[]{:S(2)}) collective-permute-start(f32[1,8,1,512]{3,2,1,0:T(1,128)S(1)} %get-tuple-element.112), channel_id=1, source_target_pairs={{8,0},{16,8},{24,16},{9,1},{17,9},{25,17},{10,2},{18,10},{26,18},{... | collective-permute-start | bytes 49160 | tf_op jit(solution)/shard_map/ppermute | solution.py:34
  81.7 55.0 %collective-permute-start.7 = (f32[1,8,1,512]{3,2,1,0:T(1,128)S(1)}, f32[1,8,1,512]{3,2,1,0:T(1,128)S(1)}, u32[]{:S(2)}, u32[]{:S(2)}) collective-permute-start(f32[1,8,1,512]{3,2,1,0:T(1,128)S(1)} %get-tuple-element.111), channel_id=1, source_target_pairs={{0,8},{8,16},{16,24},{1,9},{9,17},{17,25},{2,10},{10,18},{18,26},{... | collective-permute-start | bytes 49160 | tf_op jit(solution)/shard_map/ppermute | solution.py:32
  123.6 13.1 %copy-start.13 = (f32[1,8,112,512]{3,2,1,0:T(8,128)S(1)}, f32[1,8,112,512]{3,2,1,0:T(8,128)}, u32[]{:S(2)}) copy-start(f32[1,8,112,512]{3,2,1,0:T(8,128)} %copy-done.12) | copy-start | bytes 5505028
  131.9 6.7 %copy-start.11 = (f32[1,8,112,512]{3,2,1,0:T(8,128)}, f32[1,8,112,512]{3,2,1,0:T(8,128)S(1)}, u32[]{:S(2)}) copy-start(f32[1,8,112,512]{3,2,1,0:T(8,128)S(1)} %get-tuple-element.86) | copy-start | bytes 5505028
  132.1 18.4 %collective-permute-start.2 = (f32[1,8,112,1]{3,2,1,0:T(8,128)S(1)}, f32[1,8,112,1]{3,2,1,0:T(8,128)S(1)}, u32[]{:S(2)}, u32[]{:S(2)}) collective-permute-start(f32[1,8,112,1]{3,2,1,0:T(8,128)S(1)} %get-tuple-element.113), channel_id=1, source_target_pairs={{1,0},{2,1},{3,2},{4,3},{5,4},{6,5},{7,6},{0,7},{9,8},{10,9},{11,1... | collective-permute-start | bytes 10760 | tf_op jit(solution)/shard_map/ppermute | solution.py:34
  136.7 13.8 %collective-permute-start.3 = (f32[1,8,112,1]{3,2,1,0:T(8,128)S(1)}, f32[1,8,112,1]{3,2,1,0:T(8,128)}, u32[]{:S(2)}, u32[]{:S(2)}) collective-permute-start(f32[1,8,112,1]{3,2,1,0:T(8,128)S(1)} %get-tuple-element.114), channel_id=1, source_target_pairs={{0,1},{1,2},{2,3},{3,4},{4,5},{5,6},{6,7},{7,0},{8,9},{9,10},{10,1... | collective-permute-start | bytes 10760 | tf_op jit(solution)/shard_map/ppermute | solution.py:32
  159.0 23.3 %collective-permute-start.8 = (f32[1,4,112,512]{3,2,1,0:T(8,128)S(1)}, f32[1,4,112,512]{3,2,1,0:T(8,128)}, u32[]{:S(2)}, u32[]{:S(2)}) collective-permute-start(f32[1,4,112,512]{3,2,1,0:T(8,128)S(1)} %constant_dynamic-slice_fusion.6), channel_id=1, source_target_pairs={{0,1},{1,2},{2,3},{3,4},{4,5},{5,6},{6,7},{7,0},{8,9},{9,10},{10,1... | collective-permute-start | bytes 2752520 | tf_op jit(solution)/shard_map/ppermute | solution.py:146
  160.9 34.0 %copy-start.20 = (s32[112]{0:T(128)S(1)}, s32[112]{0:T(128)}, u32[]{:S(2)}) copy-start(s32[112]{0:T(128)} %param.21) | copy-start | bytes 1348
  160.9 34.0 %copy-start.21 = (s32[112]{0:T(128)S(1)}, s32[112]{0:T(128)}, u32[]{:S(2)}) copy-start(s32[112]{0:T(128)} %param.22) | copy-start | bytes 1348
  187.2 25.2 %collective-permute-start.9 = (f32[1,4,112,512]{3,2,1,0:T(8,128)S(1)}, f32[1,4,112,512]{3,2,1,0:T(8,128)S(1)}, u32[]{:S(2)}, u32[]{:S(2)}) collective-permute-start(f32[1,4,112,512]{3,2,1,0:T(8,128)S(1)} %get-tuple-element.99), channel_id=1, source_target_pairs={{0,2},{1,3},{2,4},{3,5},{4,6},{5,7},{6,0},{7,1},{8,10},{9,11},{10,... | collective-permute-start | bytes 2752520 | tf_op jit(solution)/shard_map/ppermute | solution.py:146
  187.2 80.6 %collective-permute-start.10 = (f32[1,4,112,512]{3,2,1,0:T(8,128)}, f32[1,4,112,512]{3,2,1,0:T(8,128)}, u32[]{:S(2)}, u32[]{:S(2)}) collective-permute-start(f32[1,4,112,512]{3,2,1,0:T(8,128)} %get-tuple-element.98), channel_id=1, source_target_pairs={{0,3},{1,4},{2,5},{3,6},{4,7},{5,0},{6,1},{7,2},{8,11},{9,12},{10,... | collective-permute-start | bytes 2752520 | tf_op jit(solution)/shard_map/ppermute | solution.py:146
  187.4 99.9 %collective-permute-start.11 = (f32[1,4,112,512]{3,2,1,0:T(8,128)}, f32[1,4,112,512]{3,2,1,0:T(8,128)}, u32[]{:S(2)}, u32[]{:S(2)}) collective-permute-start(f32[1,4,112,512]{3,2,1,0:T(8,128)} %get-tuple-element.97), channel_id=1, source_target_pairs={{0,4},{1,5},{2,6},{3,7},{4,0},{5,1},{6,2},{7,3},{8,12},{9,13},{10,... | collective-permute-start | bytes 2752520 | tf_op jit(solution)/shard_map/ppermute | solution.py:146
  190.9 98.6 %collective-permute-start.12 = (f32[1,4,112,512]{3,2,1,0:T(8,128)S(1)}, f32[1,4,112,512]{3,2,1,0:T(8,128)}, u32[]{:S(2)}, u32[]{:S(2)}) collective-permute-start(f32[1,4,112,512]{3,2,1,0:T(8,128)S(1)} %get-tuple-element.96), channel_id=1, source_target_pairs={{0,5},{1,6},{2,7},{3,0},{4,1},{5,2},{6,3},{7,4},{8,13},{9,14},{10,... | collective-permute-start | bytes 2752520 | tf_op jit(solution)/shard_map/ppermute | solution.py:146
  193.3 98.4 %collective-permute-start.13 = (f32[1,4,112,512]{3,2,1,0:T(8,128)S(1)}, f32[1,4,112,512]{3,2,1,0:T(8,128)}, u32[]{:S(2)}, u32[]{:S(2)}) collective-permute-start(f32[1,4,112,512]{3,2,1,0:T(8,128)S(1)} %get-tuple-element.95), channel_id=1, source_target_pairs={{0,6},{1,7},{2,0},{3,1},{4,2},{5,3},{6,4},{7,5},{8,14},{9,15},{10,... | collective-permute-start | bytes 2752520 | tf_op jit(solution)/shard_map/ppermute | solution.py:146
  212.4 90.8 %collective-permute-start.14 = (f32[1,4,112,512]{3,2,1,0:T(8,128)S(1)}, f32[1,4,112,512]{3,2,1,0:T(8,128)}, u32[]{:S(2)}, u32[]{:S(2)}) collective-permute-start(f32[1,4,112,512]{3,2,1,0:T(8,128)S(1)} %get-tuple-element.94), channel_id=1, source_target_pairs={{0,7},{1,0},{2,1},{3,2},{4,3},{5,4},{6,5},{7,6},{8,15},{9,8},{10,9... | collective-permute-start | bytes 2752520 | tf_op jit(solution)/shard_map/ppermute | solution.py:146
  323.6 5.3 copy-start.2
  399.6 5.2 copy-start.6
  (13 other events, 42.1 us)
